TPU v7x, 512 devices: a whole 4x8x8 slice. The times are simulated.
512 devices in a mesh: seq: 64 (over x, z, core), head: 8 (over y).
Axes of the slice: x: 4, y: 8, z: 8, core: 2. Of those that a mesh axis runs over, the one named last changes fastest.
Arguments:
- queries: bfloat16 [16384, 4096], P('seq', 'head'), may hold values from -6 to 6
- keys: bfloat16 [16384, 4096], P('seq', 'head'), may hold values from -6 to 6
- values: bfloat16 [16384, 4096], P('seq', 'head'), may hold values from -6 to 6
- gate: bfloat16 [16384, 4096], P('seq', 'head'), may hold values from -6 to 6
- residual: bfloat16 [16384, 4096], P('seq', 'head'), may hold values from -40 to 40
- log_decay: float32 [16384, 32], P('seq', 'head'), may hold values from -1 to 0, as said below
- out_weight: bfloat16 [4096, 4096], P('seq', 'head'), may hold values from -0.09375 to 0.09375
- norm_gain: bfloat16 [4096], P('head'), may hold values from 0.099609375 to 1.8984375
- kv_weight: bfloat16 [4096, 2048], P('seq', 'head'), may hold values from -0.09375 to 0.09375
Outputs:
- cache_keys: bfloat16 [16384, 1024], P('seq', 'head')
- cache_values: bfloat16 [16384, 1024], P('seq', 'head')
Inputs may be any that keep to these rules, and one draw needn't show every extreme that they name: `log_decay`: every entry is negative.
All inputs are finite; a program needn't handle non-finite values.
Results may differ from a plain program's by a relative error of at most 0.015.
Values may be sent and summed in bfloat16 or wider, within the bound.
A program may use at most 64 MiB of HBM per device.

v0:
```python
import jax
import jax.numpy as jnp
from jax import lax
from jax.sharding import PartitionSpec as P

HIGHEST = lax.Precision.HIGHEST


def entering(part, axis, combine, identity):
    place = lax.axis_index(axis)
    gathered = jax.tree.map(lambda a: lax.all_gather(a, axis), part)
    state = jax.tree.map(lambda a, e: jnp.zeros_like(a) + jnp.asarray(e, a.dtype), part, identity)

    def one(step, state):
        return combine(
            state, jax.tree.map(lambda a: lax.dynamic_index_in_dim(a, step, 0, False), gathered)
        )

    return lax.fori_loop(0, place, one, state)


def local_retention(queries, keys, values, log_decay, block):
    tokens, heads, width = queries.shape
    count = tokens // block

    def to_blocks(array):
        return array.reshape((count, block) + array.shape[1:])

    lower = jnp.arange(block)[:, None] >= jnp.arange(block)[None, :]

    def advance(carry, inputs):
        state, offset = carry
        query_block, key_block, value_block, decay_block = inputs
        within = jnp.cumsum(decay_block, axis=0)
        spread = within[:, None, :] - within[None, :, :]
        factor = jnp.where(
            lower[:, :, None], jnp.exp(jnp.where(lower[:, :, None], spread, 0.0)), 0.0
        )
        scores = jnp.einsum(
            "ihd,jhd->hij", query_block, key_block, preferred_element_type=jnp.float32
        )
        weighted = scores * jnp.transpose(factor, (2, 0, 1))
        values_wide = value_block.astype(jnp.float32)
        intra = jnp.einsum("hij,jhd->ihd", weighted, values_wide, precision=HIGHEST)
        query_wide = query_block.astype(jnp.float32)
        carried = jnp.exp(within)[:, :, None] * jnp.einsum(
            "ihd,hde->ihe", query_wide, state, precision=HIGHEST
        )
        ending = within[-1]
        key_wide = key_block.astype(jnp.float32) * jnp.exp(ending[None, :] - within)[:, :, None]
        fresh = jnp.exp(ending)[:, None, None] * state + jnp.einsum(
            "jhd,jhe->hde", key_wide, values_wide, precision=HIGHEST
        )
        return ((fresh, offset + ending), (intra + carried, offset[None, :] + within))

    start = (jnp.zeros((heads, width, width), jnp.float32), jnp.zeros((heads,), jnp.float32))
    final, stacked = lax.scan(
        advance,
        start,
        (to_blocks(queries), to_blocks(keys), to_blocks(values), to_blocks(log_decay)),
    )
    return (
        stacked[0].reshape(tokens, heads, width),
        stacked[1].reshape(tokens, heads),
        final[0],
        final[1],
    )


def combine_states(earlier, later):
    return (earlier[0] * later[0], later[0][:, None, None] * earlier[1] + later[1])


def on_device(queries, keys, values, gate, residual, log_decay, out_weight, norm_gain, kv_weight):
    tokens = queries.shape[0]
    heads = log_decay.shape[1]
    width = queries.shape[1] // heads
    shaped = [array.reshape(tokens, heads, width) for array in (queries, keys, values)]
    partial_out, running, state, offset = local_retention(
        shaped[0], shaped[1], shaped[2], log_decay, min(512, tokens)
    )
    identity = (jnp.ones((heads,), jnp.float32), jnp.zeros((heads, width, width), jnp.float32))
    scan_decay, incoming = entering((jnp.exp(offset), state), "seq", combine_states, identity)
    retained = partial_out + jnp.exp(running)[:, :, None] * jnp.einsum(
        "thd,hde->the", shaped[0].astype(jnp.float32), incoming, precision=HIGHEST
    )
    scale = lax.rsqrt(jnp.mean(retained * retained, axis=2, keepdims=True) + 1e-06)
    mixed = (
        jax.nn.silu(gate.astype(jnp.float32)) * (retained * scale).reshape(tokens, heads * width)
    ).astype(jnp.bfloat16)
    all_heads = lax.all_gather(mixed, "head", axis=1, tiled=True)
    out_full, kv_full = (
        lax.all_gather(out_weight, "seq", axis=0, tiled=True),
        lax.all_gather(kv_weight, "seq", axis=0, tiled=True),
    )
    branch = jnp.dot(all_heads, out_full, preferred_element_type=jnp.float32)
    hidden = (residual.astype(jnp.float32) + branch).astype(jnp.bfloat16)
    wide = hidden.astype(jnp.float32)
    squares = lax.psum(jnp.sum(wide * wide, axis=1), "head")
    features = wide.shape[1] * lax.axis_size("head")
    inverse = lax.rsqrt(squares[:, None] / features + 1e-06)
    local_norm = (wide * inverse * norm_gain.astype(jnp.float32)[None, :]).astype(jnp.bfloat16)
    normalized = lax.all_gather(local_norm, "head", axis=1, tiled=True)
    projected = jnp.dot(normalized, kv_full, preferred_element_type=jnp.float32)
    cache_heads = kv_weight.shape[1] // (2 * width)
    arranged = projected.reshape(tokens, cache_heads, 2, width)
    cache_keys = arranged[:, :, 0, :].reshape(tokens, cache_heads * width).astype(jnp.bfloat16)
    cache_values = arranged[:, :, 1, :].reshape(tokens, cache_heads * width).astype(jnp.bfloat16)
    return (cache_keys, cache_values)


def solution(mesh):
    placed = (
        P("seq", "head"),
        P("seq", "head"),
        P("seq", "head"),
        P("seq", "head"),
        P("seq", "head"),
        P("seq", "head"),
        P("seq", "head"),
        P("head"),
        P("seq", "head"),
    )
    return jax.shard_map(
        on_device,
        mesh=mesh,
        in_specs=placed,
        out_specs=(P("seq", "head"), P("seq", "head")),
        check_vma=False,
    )
```

profile of v0, /device:TPU:2, one launch (start us, length us, event | category | flops | bytes accessed | tf_op | source)
XLA Modules:
  0.0 390.9 jit_solution(8764286394529594663)
XLA Ops:
  8.0 1.2 reduce-window.6
  9.8 1.1 copy.73
  10.9 2.0 convolution_add_fusion.1
  13.8 44.7 %all-gather.1 = f32[64,1,4]{2,1,0:T(1,128)S(1)} all-gather(f32[1,1,4]{2,1,0:T(1,128)S(1)} %bitcast.97), channel_id=1, replica_groups=mesh['seq'=64,'head'=8] {'seq'}, dimensions={0}, use_global_device_ids=true | all-gather | bytes 1040 | tf_op jit(solution)/shard_map/all_gather | solution.py:11
  59.4 63.1 %all-gather.16.cloned.1.call-done = f32[256,128,128]{2,1,0:T(8,128)} async-done(((f32[4,128,128]{2,1,0:T(8,128)}), f32[256,128,128]{2,1,0:T(8,128)}) %all-gather.16.cloned.1.call-update) | async-done | bytes 16777232 | tf_op jit(solution)/shard_map/all_gather | solution.py:11
  122.5 17.8 %while.3 = (s32[]{:T(128)}, f32[4,128,128]{2,1,0:T(8,128)S(1)}, s32[]{:T(128)}, f32[64,4]{1,0:T(8,128)S(1)}, f32[64,4,128,128]{3,2,1,0:T(8,128)}, /*index=5*/s32[]{:T(128)}, s32[]{:T(128)}, s32[]{:T(128)}) while((s32[]{:T(128)}, f32[4,128,128]{2,1,0:T(8,128)S(1)}, s32[]{:T(128)}, f32[64,4]{1,0:T(8,128)S(1)}, f32[64,4,128,128]{3,2,1,0:T(8,128)}, ...), condition=%wide.region_3.4_spmd, body=%wide.region_2.3_spmd.sunk | while | flops 131077 | bytes 786607 | solution.py:19
  122.6 1.1 bitcast_add_fusion.2
  123.7 1.1 bitcast_add_fusion.2
  124.8 1.1 bitcast_add_fusion.2
  125.9 1.1 bitcast_add_fusion.2
  127.0 1.1 bitcast_add_fusion.2
  128.1 1.1 bitcast_add_fusion.2
  129.2 1.1 bitcast_add_fusion.2
  130.4 1.1 bitcast_add_fusion.2
  131.5 1.1 bitcast_add_fusion.2
  132.6 1.1 bitcast_add_fusion.2
  133.7 1.1 bitcast_add_fusion.2
  134.8 1.1 bitcast_add_fusion.2
  135.9 1.1 bitcast_add_fusion.2
  137.0 1.1 bitcast_add_fusion.2
  138.1 1.1 bitcast_add_fusion.2
  139.2 1.1 bitcast_add_fusion.2
  140.8 0.8 multiply_reduce_fusion.1
  141.8 0.9 fusion.12
  143.4 64.4 %all-gather.10.cloned.1.call-done = bf16[4096,512]{1,0:T(8,128)(2,1)} async-done(((bf16[64,512]{1,0:T(8,128)(2,1)}), bf16[4096,512]{1,0:T(8,128)(2,1)}) %all-gather.10.cloned.1.call-update) | async-done | bytes 4194320 | tf_op jit(solution)/shard_map/all_gather | solution.py:93
  207.8 43.4 %all-gather.8.cloned.1.call-done = bf16[256,4096]{1,0:T(8,128)(2,1)} async-done(((bf16[256,512]{1,0:T(8,128)(2,1)}), bf16[256,4096]{1,0:T(8,128)(2,1)}) %all-gather.8.cloned.1.call-update) | async-done | bytes 2097168 | tf_op jit(solution)/shard_map/all_gather | solution.py:91
  251.2 4.2 %multiply_reduce_fusion = (f32[256]{0:T(256)S(1)}, f32[256,512]{1,0:T(8,128)S(1)}) fusion(bf16[256,4096]{1,0:T(8,128)(2,1)} %all-gather.8.cloned.1.call-done, bf16[4096,512]{1,0:T(8,128)(2,1)} %all-gather.10.cloned.1.call-done, bf16[256,512]{1,0:T(8,128)(2,1)S(1)} %copy-done.4), kind=kOutput, calls=%fused_computation.22 | convolution fusion | flops 1074528000 | bytes 7078912 | tf_op jit(solution)/shard_map/dot_general | solution.py:96
  255.3 16.2 %psum.7 = f32[256]{0:T(256)S(1)} all-reduce(f32[256]{0:T(256)S(1)} %get-tuple-element.97), channel_id=1, replica_groups=mesh['seq'=64,'head'=8] {'head'}, use_global_device_ids=true, to_apply=%region_6.7 | all-reduce | flops 256 | bytes 2048 | tf_op jit(solution)/shard_map/psum | solution.py:99
  271.6 0.8 multiply_convert_fusion
  272.4 63.8 %all-gather.14.cloned.1.call-done = bf16[4096,256]{1,0:T(8,128)(2,1)} async-done(((bf16[64,256]{1,0:T(8,128)(2,1)}), bf16[4096,256]{1,0:T(8,128)(2,1)}) %all-gather.14.cloned.1.call-update) | async-done | bytes 2097168 | tf_op jit(solution)/shard_map/all_gather | solution.py:94
  336.2 43.6 %all-gather.12.cloned.1.call-done = bf16[256,4096]{1,0:T(8,128)(2,1)} async-done(((bf16[256,512]{1,0:T(8,128)(2,1)}), bf16[256,4096]{1,0:T(8,128)(2,1)}) %all-gather.12.cloned.1.call-update) | async-done | bytes 2097168 | tf_op jit(solution)/shard_map/all_gather | solution.py:103
  379.8 3.1 convolution_convert_fusion
  (60 shorter events, 6.0 us)
Async XLA Ops:
  7.2 51.4 %copy-start = (bf16[256,512]{1,0:T(8,128)(2,1)S(1)}, bf16[256,512]{1,0:T(8,128)(2,1)}, u32[]{:S(2)}) copy-start(bf16[256,512]{1,0:T(8,128)(2,1)} %param.11) | copy-start | bytes 786436
  7.2 115.3 %all-gather.16.cloned.1.call-start = ((), (), s32[]{:S(2)}) async-start(), calls=%async_computation.4 | async-start | bytes 17039360 | tf_op jit(solution)/shard_map/all_gather | solution.py:11
  13.0 194.8 %all-gather.10.cloned.1.call-start = ((), (), s32[]{:S(2)}) async-start(), calls=%async_computation.1 | async-start | bytes 4259840 | tf_op jit(solution)/shard_map/all_gather | solution.py:93
  13.8 237.4 %all-gather.8.cloned.1.call-start = ((), (), s32[]{:S(2)}) async-start(), calls=%async_computation | async-start | bytes 2359296 | tf_op jit(solution)/shard_map/all_gather | solution.py:91
  122.5 18.2 %copy-start.1 = (bf16[256,512]{1,0:T(8,128)(2,1)S(1)}, bf16[256,512]{1,0:T(8,128)(2,1)}, u32[]{:S(2)}) copy-start(bf16[256,512]{1,0:T(8,128)(2,1)} %param.13) | copy-start | bytes 786436
  140.8 1.1 copy-start.2
  141.5 1.8 copy-start.3
  141.5 109.7 %copy-start.4 = (bf16[256,512]{1,0:T(8,128)(2,1)S(1)}, bf16[256,512]{1,0:T(8,128)(2,1)}, u32[]{:S(2)}) copy-start(bf16[256,512]{1,0:T(8,128)(2,1)} %param.15) | copy-start | bytes 786436
  142.7 193.4 %all-gather.14.cloned.1.call-start = ((), (), s32[]{:S(2)}) async-start(), calls=%async_computation.3 | async-start | bytes 2129920 | tf_op jit(solution)/shard_map/all_gather | solution.py:94
  143.3 236.5 %all-gather.12.cloned.1.call-start = ((), (), s32[]{:S(2)}) async-start(), calls=%async_computation.2 | async-start | bytes 2359296 | tf_op jit(solution)/shard_map/all_gather | solution.py:103
Sparse Core Ops, SparseCore 0:
  13.1 109.3 all-gather.15
  125.8 81.8 all-gather.9
  209.9 41.2 all-gather.7
  254.4 81.7 all-gather.13
  338.1 41.6 all-gather.11
where the time goes:
time: 393 us; the launch traced here: 391 us
  waiting for transfers between devices  280 us (71%)
  blocking collectives  60.9 us (15%)
  other arithmetic  20.2 us (5%)
  between operations  14 us (4%)
  matrix products  11.3 us (3%)
  local copies, waits for them, and re-layouts  4.19 us (1%)
    all_gather x1, waiting for transfers between devices, on_device(): lax.all_gather(out_weight, 'seq', axis=0, tiled=True)  64.4 us
    all_gather x1, waiting for transfers between devices, on_device(): lax.all_gather(kv_weight, 'seq', axis=0, tiled=True)  63.8 us
    all_gather x1, waiting for transfers between devices, entering(): gathered = jax.tree.map(lambda a: lax.all_gather(a, axis), part)  63.1 us
    all_gather x1, blocking collectives, entering(): gathered = jax.tree.map(lambda a: lax.all_gather(a, axis), part)  44.7 us
    all_gather x1, waiting for transfers between devices, on_device(): normalized = lax.all_gather(local_norm, 'head', axis=1, tiled=True)  43.6 us
    all_gather x1, waiting for transfers between devices, on_device(): all_heads = lax.all_gather(mixed, 'head', axis=1, tiled=True)  43.4 us
    add x16, other arithmetic, combine_states(): later[0][:, None, None] * earlier[1] + later[1]  17 us
    psum x1, blocking collectives, on_device(): squares = lax.psum(jnp.sum(wide * wide, axis=1), 'head')  16.2 us
  transfers between devices with their start and end apart: 5, of which 5 were waited for; matrix products, arithmetic and copies ran while one was open for 6% of the time, Pallas kernels for 0%

commit v1 on v0

--- a/solution.py
+++ b/solution.py
@@ -4,6 +4,15 @@
 from jax.sharding import PartitionSpec as P
 
 HIGHEST = lax.Precision.HIGHEST
+outputs_bind = lambda obj: jnp.concatenate(
+    lax.all_to_all(
+        jnp.stack([obj for _ in range(lax.axis_size("seq"))]),
+        axis_name="seq",
+        split_axis=0,
+        concat_axis=0,
+    ),
+    axis=0,
+)
 
 
 def entering(part, axis, combine, identity):
@@ -90,7 +99,7 @@
     ).astype(jnp.bfloat16)
     all_heads = lax.all_gather(mixed, "head", axis=1, tiled=True)
     out_full, kv_full = (
-        lax.all_gather(out_weight, "seq", axis=0, tiled=True),
+        outputs_bind(out_weight),
         lax.all_gather(kv_weight, "seq", axis=0, tiled=True),
     )
     branch = jnp.dot(all_heads, out_full, preferred_element_type=jnp.float32)

time: 393 us -> 439 us (1.12)
  blocking collectives: 60.9 us -> 172 us
  waiting for transfers between devices: 280 us -> 197 us
  starting transfers between devices: 0.2 us -> 14.2 us
    all_gather x1, blocking collectives: 44.7 us -> 156 us  [entering(): gathered = jax.tree.map(lambda a: lax.all_gather(a, axis), part)]
    all_gather x1 -> x0, waiting for transfers between devices: 64.4 us -> none  [on_device(): lax.all_gather(out_weight, 'seq', axis=0, tiled=True)]
    all_gather x1, waiting for transfers between devices: 63.1 us -> 0.02 us  [entering(): gathered = jax.tree.map(lambda a: lax.all_gather(a, axis), part)]
    all_gather x1, waiting for transfers between devices: 43.4 us -> 89 us  [on_device(): all_heads = lax.all_gather(mixed, 'head', axis=1, tiled=True)]
    all_to_all x0 -> x1, starting transfers between devices: none -> 14.1 us  [lax.all_to_all(jnp.stack([obj for _ in range(lax.axis_size('seq'))]), axi...]
  transfers between devices with their start and end apart: 5 -> 5, of which waited for: 5 -> 3; matrix products, arithmetic and copies ran while one was open for 6% -> 7% of each run, Pallas kernels for 0% -> 0%
where the time goes in v1:
time: 439 us; the launch traced here: 437 us
  waiting for transfers between devices  197 us (45%)
  blocking collectives  172 us (39%)
  other arithmetic  20.2 us (5%)
  starting transfers between devices  14.2 us (3%)
  between operations  14 us (3%)
  matrix products  11.3 us (3%)
  local copies, waits for them, and re-layouts  7.5 us (2%)
    all_gather x1, blocking collectives, entering(): gathered = jax.tree.map(lambda a: lax.all_gather(a, axis), part)  156 us
    all_gather x1, waiting for transfers between devices, on_device(): all_heads = lax.all_gather(mixed, 'head', axis=1, tiled=True)  89 us
    all_gather x1, waiting for transfers between devices, on_device(): lax.all_gather(kv_weight, 'seq', axis=0, tiled=True)  63.9 us
    all_gather x1, waiting for transfers between devices, on_device(): normalized = lax.all_gather(local_norm, 'head', axis=1, tiled=True)  43.6 us
    add x16, other arithmetic, combine_states(): later[0][:, None, None] * earlier[1] + later[1]  17 us
    psum x1, blocking collectives, on_device(): squares = lax.psum(jnp.sum(wide * wide, axis=1), 'head')  16.2 us
    all_to_all x1, starting transfers between devices, lax.all_to_all(jnp.stack([obj for _ in range(lax.axis_size('seq'))]), axi...  14.1 us
  transfers between devices with their start and end apart: 5, of which 3 were waited for; matrix products, arithmetic and copies ran while one was open for 7% of the time, Pallas kernels for 0%

profile of v1, /device:TPU:2, one launch (start us, length us, event | category | flops | bytes accessed | tf_op | source)
XLA Modules:
  0.0 436.9 jit_solution(14107692007055989667)
XLA Ops:
  8.0 1.2 reduce-window.6
  9.8 1.1 copy.73
  10.9 2.1 convolution_add_fusion.1
  13.0 3.3 stack.2
  16.3 14.1 %all-to-all-start = ((bf16[64,64,512]{2,1,0:T(8,128)(2,1)}), bf16[64,64,512]{2,1,0:T(8,128)(2,1)}, u32[]{:S(2)}, u32[]{:S(2)}) async-start(bf16[64,64,512]{2,1,0:T(8,128)(2,1)} %stack.2), calls=%async_computation | async-start | bytes 8388608 | tf_op jit(solution)/shard_map/all_to_all | solution.py:8
  30.5 155.7 %all-gather.1 = f32[64,1,4]{2,1,0:T(1,128)S(1)} all-gather(f32[1,1,4]{2,1,0:T(1,128)S(1)} %bitcast.98), channel_id=1, replica_groups=mesh['seq'=64,'head'=8] {'seq'}, dimensions={0}, use_global_device_ids=true | all-gather | bytes 1040 | tf_op jit(solution)/shard_map/all_gather | solution.py:20
  187.0 17.7 %while.3 = (s32[]{:T(128)}, f32[4,128,128]{2,1,0:T(8,128)S(1)}, s32[]{:T(128)}, f32[64,4]{1,0:T(8,128)S(1)}, f32[64,4,128,128]{3,2,1,0:T(8,128)}, /*index=5*/s32[]{:T(128)}, s32[]{:T(128)}, s32[]{:T(128)}) while((s32[]{:T(128)}, f32[4,128,128]{2,1,0:T(8,128)S(1)}, s32[]{:T(128)}, f32[64,4]{1,0:T(8,128)S(1)}, f32[64,4,128,128]{3,2,1,0:T(8,128)}, ...), condition=%wide.region_3.4_spmd, body=%wide.region_2.3_spmd.sunk | while | flops 131077 | bytes 786607 | solution.py:28
  187.1 1.1 bitcast_add_fusion.2
  188.2 1.1 bitcast_add_fusion.2
  189.3 1.1 bitcast_add_fusion.2
  190.4 1.1 bitcast_add_fusion.2
  191.5 1.1 bitcast_add_fusion.2
  192.6 1.1 bitcast_add_fusion.2
  193.7 1.1 bitcast_add_fusion.2
  194.9 1.1 bitcast_add_fusion.2
  196.0 1.1 bitcast_add_fusion.2
  197.1 1.1 bitcast_add_fusion.2
  198.2 1.1 bitcast_add_fusion.2
  199.3 1.1 bitcast_add_fusion.2
  200.4 1.1 bitcast_add_fusion.2
  201.5 1.1 bitcast_add_fusion.2
  202.6 1.1 bitcast_add_fusion.2
  203.7 1.1 bitcast_add_fusion.2
  205.2 0.8 multiply_reduce_fusion.1
  206.3 0.9 fusion.12
  208.0 89.0 %all-gather.7.cloned.1.call-done = bf16[256,4096]{1,0:T(8,128)(2,1)} async-done(((bf16[256,512]{1,0:T(8,128)(2,1)}), bf16[256,4096]{1,0:T(8,128)(2,1)}) %all-gather.7.cloned.1.call-update) | async-done | bytes 2097168 | tf_op jit(solution)/shard_map/all_gather | solution.py:100
  297.0 4.1 multiply_reduce_fusion
  301.1 16.2 %psum.7 = f32[256]{0:T(256)S(1)} all-reduce(f32[256]{0:T(256)S(1)} %get-tuple-element.97), channel_id=1, replica_groups=mesh['seq'=64,'head'=8] {'head'}, use_global_device_ids=true, to_apply=%region_6.7 | all-reduce | flops 256 | bytes 2048 | tf_op jit(solution)/shard_map/psum | solution.py:108
  317.4 0.8 multiply_convert_fusion
  318.2 63.9 %all-gather.11.cloned.1.call-done = bf16[4096,256]{1,0:T(8,128)(2,1)} async-done(((bf16[64,256]{1,0:T(8,128)(2,1)}), bf16[4096,256]{1,0:T(8,128)(2,1)}) %all-gather.11.cloned.1.call-update) | async-done | bytes 2097168 | tf_op jit(solution)/shard_map/all_gather | solution.py:103
  382.1 43.6 %all-gather.9.cloned.1.call-done = bf16[256,4096]{1,0:T(8,128)(2,1)} async-done(((bf16[256,512]{1,0:T(8,128)(2,1)}), bf16[256,4096]{1,0:T(8,128)(2,1)}) %all-gather.9.cloned.1.call-update) | async-done | bytes 2097168 | tf_op jit(solution)/shard_map/all_gather | solution.py:112
  425.7 3.1 convolution_convert_fusion
  (60 shorter events, 5.5 us)
Async XLA Ops:
  7.2 179.0 %copy-start = (bf16[256,512]{1,0:T(8,128)(2,1)S(1)}, bf16[256,512]{1,0:T(8,128)(2,1)}, u32[]{:S(2)}) copy-start(bf16[256,512]{1,0:T(8,128)(2,1)} %param.11) | copy-start | bytes 786436
  7.2 179.8 %all-gather.13.cloned.1.call-start = ((), (), s32[]{:S(2)}) async-start(), calls=%async_computation.4 | async-start | bytes 17039360 | tf_op jit(solution)/shard_map/all_gather | solution.py:20
  16.3 191.6 %all-to-all-start = ((bf16[64,64,512]{2,1,0:T(8,128)(2,1)}), bf16[64,64,512]{2,1,0:T(8,128)(2,1)}, u32[]{:S(2)}, u32[]{:S(2)}) async-start(bf16[64,64,512]{2,1,0:T(8,128)(2,1)} %stack.2), calls=%async_computation | async-start | bytes 8388608 | tf_op jit(solution)/shard_map/all_to_all | solution.py:8
  30.4 266.6 %all-gather.7.cloned.1.call-start = ((), (), s32[]{:S(2)}) async-start(), calls=%async_computation.1 | async-start | bytes 2359296 | tf_op jit(solution)/shard_map/all_gather | solution.py:100
  187.0 18.2 %copy-start.1 = (bf16[256,512]{1,0:T(8,128)(2,1)S(1)}, bf16[256,512]{1,0:T(8,128)(2,1)}, u32[]{:S(2)}) copy-start(bf16[256,512]{1,0:T(8,128)(2,1)} %param.13) | copy-start | bytes 786436
  205.2 1.1 copy-start.2
  206.0 2.0 copy-start.3
  206.0 91.0 %copy-start.4 = (bf16[256,512]{1,0:T(8,128)(2,1)S(1)}, bf16[256,512]{1,0:T(8,128)(2,1)}, u32[]{:S(2)}) copy-start(bf16[256,512]{1,0:T(8,128)(2,1)} %param.15) | copy-start | bytes 786436
  207.2 174.9 %all-gather.11.cloned.1.call-start = ((), (), s32[]{:S(2)}) async-start(), calls=%async_computation.3 | async-start | bytes 2129920 | tf_op jit(solution)/shard_map/all_gather | solution.py:103
  207.9 217.8 %all-gather.9.cloned.1.call-start = ((), (), s32[]{:S(2)}) async-start(), calls=%async_computation.2 | async-start | bytes 2359296 | tf_op jit(solution)/shard_map/all_gather | solution.py:112
Sparse Core Ops, SparseCore 0:
  13.2 161.8 all-gather.12
  207.3 89.6 all-gather.6
  300.4 81.7 all-gather.10
  384.0 41.6 all-gather.8
